TPU v7x, 256 devices: a whole 4x4x8 slice. The times are simulated.
256 devices in a mesh: batch: 128 (over y, z, x), tile: 2 (over core).
Axes of the slice: x: 4, y: 4, z: 8, core: 2. Of those that a mesh axis runs over, the one named last changes fastest.
Arguments:
- first_view: bfloat16 [256, 8192], P('batch'), may hold values from -1500 to 1500
- second_view: bfloat16 [256, 8192], P('batch'), may hold values from -1500 to 1500
Outputs:
- grad_first: bfloat16 [256, 8192], P('batch', 'tile')
- grad_second: bfloat16 [256, 8192], P('batch', 'tile')
All inputs are finite; a program needn't handle non-finite values.
Results may differ from a plain program's by a relative error of at most 0.0043.
Values may be sent and summed in bfloat16 or wider, within the bound.
A program may use at most 64 MiB of HBM per device.

v0:
```python
import jax
import jax.numpy as jnp
from jax import lax
from jax.sharding import PartitionSpec as P

BAND = 16


epsilon = 1e-05
decorrelation = 0.0051


def fold_rows(received, row_count, row_groups, group_size, block_width):
    return (
        received.reshape(row_count, row_groups, group_size, block_width)
        .sum(2)
        .reshape(row_count, row_groups * block_width)
    )


def fold_cols(received, row_count, row_groups, group_size, block_width):
    return (
        received.reshape(row_count, row_groups, group_size, block_width)
        .sum(1)
        .reshape(row_count, group_size * block_width)
    )


def per_device(first_view, second_view):
    row_count, feature_width = first_view.shape
    device_count = lax.axis_size("batch")
    band_index = lax.axis_index("batch")
    tile_index = lax.axis_index("tile")
    total_rows = row_count * device_count
    half_width = feature_width // 2
    first_float = first_view.astype(jnp.float32)
    second_float = second_view.astype(jnp.float32)
    moments = lax.psum(
        (
            jnp.sum(first_float, 0),
            jnp.sum(first_float * first_float, 0),
            jnp.sum(second_float, 0),
            jnp.sum(second_float * second_float, 0),
        ),
        "batch",
    )
    mean_first = moments[0] / total_rows
    inverse_first = lax.rsqrt(moments[1] / total_rows - mean_first * mean_first + epsilon)
    mean_second = moments[2] / total_rows
    inverse_second = lax.rsqrt(moments[3] / total_rows - mean_second * mean_second + epsilon)
    norm_first = ((first_float - mean_first) * inverse_first).astype(jnp.bfloat16)
    norm_second = ((second_float - mean_second) * inverse_second).astype(jnp.bfloat16)
    group_size = BAND
    row_groups = device_count // group_size
    block_rows = feature_width * group_size // device_count
    block_cols = feature_width // (2 * group_size)
    row_band = band_index // group_size
    column_block = band_index % group_size + group_size * tile_index
    send_first = jnp.broadcast_to(
        norm_first.reshape(row_count, row_groups, 1, block_rows),
        (row_count, row_groups, group_size, block_rows),
    ).reshape(row_count, device_count * block_rows)
    picked = lax.dynamic_slice_in_dim(
        norm_second.reshape(row_count, 2, group_size, block_cols), tile_index, 1, 1
    )
    send_second = jnp.broadcast_to(picked, (row_count, row_groups, group_size, block_cols)).reshape(
        row_count, device_count * block_cols
    )
    whole_first, whole_second = (
        lax.all_to_all(send_first, "batch", split_axis=1, concat_axis=0, tiled=True),
        lax.all_to_all(send_second, "batch", split_axis=1, concat_axis=0, tiled=True),
    )
    correlation = (
        lax.dot_general(
            whole_first, whole_second, (((0,), (0,)), ((), ())), preferred_element_type=jnp.float32
        )
        / total_rows
    )
    row_ids = row_band * block_rows + lax.iota(jnp.int32, block_rows)
    col_ids = column_block * block_cols + lax.iota(jnp.int32, block_cols)
    on_diagonal = row_ids[:, None] == col_ids[None, :]
    slope_tile = jnp.where(on_diagonal, correlation - 1.0, decorrelation * correlation).astype(
        jnp.bfloat16
    )
    pull_first = lax.dot_general(
        whole_second, slope_tile, (((1,), (1,)), ((), ())), preferred_element_type=jnp.float32
    )
    pull_second = jnp.dot(whole_first, slope_tile, preferred_element_type=jnp.float32)
    half_start = tile_index * half_width
    norm_first_half = lax.dynamic_slice_in_dim(norm_first, half_start, half_width, 1).astype(
        jnp.float32
    )
    norm_second_half = lax.dynamic_slice_in_dim(norm_second, half_start, half_width, 1).astype(
        jnp.float32
    )
    inverse_first_half = lax.dynamic_slice_in_dim(inverse_first, half_start, half_width, 0)
    inverse_second_half = lax.dynamic_slice_in_dim(inverse_second, half_start, half_width, 0)
    back_first, back_second = (
        lax.all_to_all(pull_first, "batch", split_axis=0, concat_axis=1, tiled=True),
        lax.all_to_all(pull_second, "batch", split_axis=0, concat_axis=1, tiled=True),
    )
    full_first = fold_rows(back_first, row_count, row_groups, group_size, block_rows)
    pull_second_half = fold_cols(back_second, row_count, row_groups, group_size, block_cols)
    pull_first_half = lax.psum_scatter(full_first, "tile", scatter_dimension=1, tiled=True)
    column_sums = lax.psum(
        (
            jnp.sum(pull_first_half * norm_first_half, 0, keepdims=True),
            jnp.sum(pull_second_half * norm_second_half, 0, keepdims=True),
        ),
        "batch",
    )
    stat_first = column_sums[0] / total_rows
    stat_second = column_sums[1] / total_rows
    grad_first = (inverse_first_half * (pull_first_half - norm_first_half * stat_first)).astype(
        jnp.bfloat16
    )
    grad_second = (
        inverse_second_half * (pull_second_half - norm_second_half * stat_second)
    ).astype(jnp.bfloat16)
    return (grad_first, grad_second)


def solution(mesh):
    return jax.shard_map(
        per_device,
        mesh=mesh,
        in_specs=(P("batch", None), P("batch", None)),
        out_specs=(P("batch", "tile"), P("batch", "tile")),
        check_vma=False,
    )
```

profile of v0, /device:TPU:0, one launch (start us, length us, event | category | flops | bytes accessed | tf_op | source)
XLA Modules:
  0.0 1036.5 jit_solution(13418832312192321948)
XLA Ops:
  7.2 1.5 convert_reduce_fusion.1
  8.7 1.5 convert_reduce_fusion
  10.3 217.0 %all-reduce.4.cloned.1.call-done = (f32[8192]{0:T(1024)}, f32[8192]{0:T(1024)}, f32[8192]{0:T(1024)}, f32[8192]{0:T(1024)}) async-done(((f32[8192]{0:T(1024)}, f32[8192]{0:T(1024)}, f32[8192]{0:T(1024)}, f32[8192]{0:T(1024)}), (f32[8192]{0:T(1024)}, f32[8192]{0:T(1024)}, f32[8192]{0:T(1024)}, f32[8192]{0:T(1024)})) %all-reduce.4.cloned.1.call-update) | async-done | bytes 131088 | tf_op jit(solution)/shard_map/psum | solution.py:38
  227.3 0.8 broadcast_multiply_fusion
  228.1 0.8 fusion.11
  229.0 1.3 copy.30
  230.3 10.2 all-to-all-start.1
  240.6 0.8 fusion.13
  241.4 14.9 %all-to-all-done.1 = bf16[2,128,1024]{2,0,1:T(2,128)(2,1)S(1)} async-done(((bf16[2,128,1024]{2,0,1:T(2,128)(2,1)}), bf16[2,128,1024]{2,0,1:T(2,128)(2,1)S(1)}, u32[]{:S(2)}, u32[]{:S(2)}) %all-to-all-start.1) | async-done | bytes 524320 | tf_op jit(solution)/shard_map/all_to_all | solution.py:70
  256.3 0.7 broadcast_in_dim.13
  257.1 6.3 all-to-all-start
  264.0 11.5 %all-to-all-done = bf16[2,128,256]{2,0,1:T(2,128)(2,1)S(1)} async-done(((bf16[2,128,256]{2,0,1:T(2,128)(2,1)}), bf16[2,128,256]{2,0,1:T(2,128)(2,1)S(1)}, u32[]{:S(2)}, u32[]{:S(2)}) %all-to-all-start) | async-done | bytes 131104 | tf_op jit(solution)/shard_map/all_to_all | solution.py:71
  276.2 1.8 copy.32
  278.0 6.2 all-to-all-start.2
  284.5 0.9 copy.34
  285.4 22.4 %all-to-all-done.2 = f32[128,2,1024]{2,1,0:T(2,128)S(1)} async-done(((f32[128,2,1024]{2,1,0:T(2,128)}), f32[128,2,1024]{2,1,0:T(2,128)S(1)}, u32[]{:S(2)}, u32[]{:S(2)}) %all-to-all-start.2) | async-done | bytes 1048608 | tf_op jit(solution)/shard_map/all_to_all | solution.py:99
  307.9 7.0 all-to-all-start.3
  315.1 2.6 copy.38
  317.8 10.1 all-to-all-done.3
  328.1 9.0 reduce-scatter.4.cloned.1.call-done
  337.0 2.2 copy.39
  339.3 689.0 %all-reduce = (f32[1,4096]{1,0:T(1,128)S(1)}, f32[1,4096]{1,0:T(1,128)S(1)}) all-reduce(f32[1,4096]{1,0:T(1,128)S(1)} %bitcast.62, f32[1,4096]{1,0:T(1,128)S(1)} %bitcast.60), channel_id=1, replica_groups=mesh['batch'=128,'tile'=2] {'batch'}, use_global_device_ids=true, to_apply=%region_11.12 | all-reduce | flops 8192 | bytes 65536 | tf_op jit(solution)/shard_map/psum | solution.py:105
  1028.3 0.6 fusion.18
  1029.0 0.6 fusion.22
  (23 shorter events, 2.3 us)
Async XLA Ops:
  7.2 220.1 %all-reduce.4.cloned.1.call-start = ((), (), s32[]{:S(2)}) async-start(), calls=%async_computation.6 | async-start | bytes 262144 | tf_op jit(solution)/shard_map/psum | solution.py:38
  230.3 26.0 %all-to-all-start.1 = ((bf16[2,128,1024]{2,0,1:T(2,128)(2,1)}), bf16[2,128,1024]{2,0,1:T(2,128)(2,1)S(1)}, u32[]{:S(2)}, u32[]{:S(2)}) async-start(bf16[2,128,1024]{2,0,1:T(2,128)(2,1)} %copy.30), calls=%async_computation.1 | async-start | bytes 1048576 | tf_op jit(solution)/shard_map/all_to_all | solution.py:70
  257.1 18.4 %all-to-all-start = ((bf16[2,128,256]{2,0,1:T(2,128)(2,1)}), bf16[2,128,256]{2,0,1:T(2,128)(2,1)S(1)}, u32[]{:S(2)}, u32[]{:S(2)}) async-start(bf16[2,128,256]{2,0,1:T(2,128)(2,1)} %bitcast.1), calls=%async_computation | async-start | bytes 262144 | tf_op jit(solution)/shard_map/all_to_all | solution.py:71
  278.0 29.9 %all-to-all-start.2 = ((f32[128,2,1024]{2,1,0:T(2,128)}), f32[128,2,1024]{2,1,0:T(2,128)S(1)}, u32[]{:S(2)}, u32[]{:S(2)}) async-start(f32[128,2,1024]{2,1,0:T(2,128)} %copy.32), calls=%async_computation.2 | async-start | bytes 2097152 | tf_op jit(solution)/shard_map/all_to_all | solution.py:99
  307.9 20.1 %all-to-all-start.3 = ((f32[128,2,256]{2,1,0:T(2,128)}), f32[128,2,256]{2,1,0:T(2,128)S(1)}, u32[]{:S(2)}, u32[]{:S(2)}) async-start(f32[128,2,256]{2,1,0:T(2,128)} %copy.34), calls=%async_computation.3 | async-start | bytes 524288 | tf_op jit(solution)/shard_map/all_to_all | solution.py:100
  314.8 22.2 %reduce-scatter.4.cloned.1.call-start = ((), (), s32[]{:S(2)}) async-start(), calls=%async_computation.5 | async-start | bytes 6291456
Sparse Core Ops, SparseCore 0:
  13.7 213.4 all-reduce.3
  318.4 18.5 reduce-scatter.3
where the time goes:
time: 1040 us
  blocking collectives  689 us (66%)
  waiting for transfers between devices  285 us (27%)
  starting transfers between devices  29.8 us (3%)
  between operations  14.3 us (1%)
    psum x1, blocking collectives, per_device(): lax.psum((jnp.sum(pull_first_half * norm_first_half, 0, keepdims=True), j...  689 us
    psum x1, waiting for transfers between devices, per_device(): lax.psum((jnp.sum(first_float, 0), jnp.sum(first_float * first_float, 0),...  217 us
    all_to_all x1, waiting for transfers between devices, per_device(): lax.all_to_all(pull_first, 'batch', split_axis=0, concat_axis=1, tiled=True)  22.4 us
  transfers between devices with their start and end apart: 6, of which 6 were waited for; matrix products, arithmetic and copies ran while one was open for 1% of the time, Pallas kernels for 0%

commit v1 on v0

v1 whole, which is shorter than its diff:
```python
import functools

import jax
import jax.numpy as jnp
from jax import lax
from jax.experimental import pallas as pl
from jax.experimental.pallas import tpu as pltpu
from jax.sharding import PartitionSpec as P

epsilon = 1e-05
decorrelation = 0.0051

NY, NZ, NX = 4, 8, 4
PLANE = NY * NX
MESH = pl.DeviceIdType.MESH


def kernel(
    first_ref,
    second_ref,
    grad_first_ref,
    grad_second_ref,
    piece,
    line,
    whole,
    norm,
    gram_out,
    gram_in,
    core_out,
    core_in,
    stat_out,
    stat_in,
    grad_out,
    send_sem,
    recv_sem,
):
    batch = lax.axis_index("batch")
    tile = lax.axis_index("tile")
    x = batch % NX
    z = (batch // NX) % NZ
    y = batch // (NX * NZ)
    slot = y * NX + x
    width = piece.shape[-1]
    half = width * NZ
    rows = line.shape[1]
    total_rows = rows * PLANE

    def line_peer(k):
        other = (z + k) % NZ
        return other, ((y * NZ + other) * NX + x, tile)

    def plane_peer(j, i):
        return ((((y + j) % NY) * NZ + z) * NX + (x + i) % NX, tile)

    line_steps = [4, 3, 5, 2, 6, 1, 7]
    plane_steps = [(j, i) for j in (2, 1, 3, 0) for i in (2, 1, 3, 0) if i or j]
    sibling = (batch, 1 - tile)

    barrier = pltpu.get_barrier_semaphore()
    for k in line_steps:
        pl.semaphore_signal(barrier, inc=1, device_id=line_peer(k)[1], device_id_type=MESH)
    for j, i in plane_steps:
        pl.semaphore_signal(barrier, inc=1, device_id=plane_peer(j, i), device_id_type=MESH)
    pl.semaphore_signal(barrier, inc=1, device_id=sibling, device_id_type=MESH)
    pl.semaphore_wait(barrier, len(line_steps) + len(plane_steps) + 1)

    def send(phase, source, target, device):
        pltpu.make_async_remote_copy(
            src_ref=source,
            dst_ref=target,
            send_sem=send_sem.at[phase],
            recv_sem=recv_sem.at[phase],
            device_id=device,
            device_id_type=MESH,
        ).start()

    def wait(sems, phase, like):
        pltpu.make_async_copy(like, like, sems.at[phase]).wait()

    views = (first_ref, second_ref)
    for k in line_steps:
        other, device = line_peer(k)
        start = pl.multiple_of(tile * half + other * width, width)
        for v in range(2):
            send(0, views[v].at[:, pl.ds(start, width)], piece.at[z, v], device)
    start = pl.multiple_of(tile * half + z * width, width)
    for v in range(2):
        pltpu.make_async_copy(
            views[v].at[:, pl.ds(start, width)], piece.at[z, v], recv_sem.at[0]
        ).start()
    wait(recv_sem, 0, piece)
    for v in range(2):
        line[v] = piece[:, v].astype(jnp.float32).reshape(rows, width).astype(jnp.bfloat16)

    for j, i in plane_steps:
        send(1, line, whole.at[slot], plane_peer(j, i))
    whole[slot] = line[...]
    wait(recv_sem, 1, whole.at[pl.ds(0, PLANE - 1)])

    inverse = []
    for v in range(2):
        values = whole[:, v].astype(jnp.float32).reshape(total_rows, width)
        mean = jnp.sum(values, 0, keepdims=True) / total_rows
        centered = values - mean
        variance = jnp.sum(centered * centered, 0, keepdims=True) / total_rows
        inverse.append(lax.rsqrt(variance + epsilon))
        norm[v] = (centered * inverse[v]).astype(jnp.bfloat16).reshape(PLANE, rows, width)
    for v in range(2):
        gram_out[v] = lax.dot_general(
            norm[v, slot],
            norm[v].reshape(total_rows, width),
            (((1,), (1,)), ((), ())),
            preferred_element_type=jnp.float32,
        ).astype(jnp.bfloat16)

    for k in line_steps:
        send(2, gram_out, gram_in.at[z], line_peer(k)[1])
    gram_in[z] = gram_out[...]
    norm_first = norm[0].reshape(total_rows, width)
    norm_second = norm[1].reshape(total_rows, width)
    paired = (
        jnp.sum(norm_first.astype(jnp.float32) * norm_second.astype(jnp.float32), 0, keepdims=True)
        / total_rows
    )
    excess = (paired - 1.0) - decorrelation * paired
    wait(recv_sem, 2, gram_in.at[pl.ds(0, NZ - 1)])
    core_out[...] = jnp.sum(gram_in[...].astype(jnp.float32), 0)

    send(3, core_out, core_in, sibling)
    wait(recv_sem, 3, core_in)
    gram = (core_out[...] + core_in[...]) * (decorrelation / total_rows)

    pulls = []
    mine = [norm[v, slot].astype(jnp.float32) for v in range(2)]
    for v in range(2):
        high = gram[1 - v].astype(jnp.bfloat16)
        low = (gram[1 - v] - high.astype(jnp.float32)).astype(jnp.bfloat16)
        both = jnp.dot(
            jnp.concatenate([high, low], 0),
            (norm_first, norm_second)[v],
            preferred_element_type=jnp.float32,
        )
        pull = both[:rows] + both[rows:] + excess * mine[1 - v]
        pulls.append(pull)
        stat_out[v : v + 1] = jnp.sum(pull * mine[v], 0, keepdims=True)

    for j, i in plane_steps:
        send(4, stat_out, stat_in.at[slot], plane_peer(j, i))
    stat_in[slot] = stat_out[...]
    wait(recv_sem, 4, stat_in.at[pl.ds(0, PLANE - 1)])
    stat = jnp.sum(stat_in[...], 0) / total_rows
    for v in range(2):
        grad = inverse[v] * (pulls[v] - mine[v] * stat[v : v + 1])
        grad_out[:, v] = grad.reshape(NZ, rows // NZ, width).astype(jnp.bfloat16)

    grads = (grad_first_ref, grad_second_ref)
    start = pl.multiple_of(z * width, width)
    for k in line_steps:
        other, device = line_peer(k)
        for v in range(2):
            send(5 + v, grad_out.at[other, v], grads[v].at[:, pl.ds(start, width)], device)
    for v in range(2):
        pltpu.make_async_copy(
            grad_out.at[z, v], grads[v].at[:, pl.ds(start, width)], recv_sem.at[5 + v]
        ).start()
    for v in range(2):
        wait(recv_sem, 5 + v, grads[v])

    wait(send_sem, 0, piece.at[pl.ds(0, NZ - 1)])
    wait(send_sem, 1, whole.at[pl.ds(0, PLANE - 1)])
    wait(send_sem, 2, gram_in.at[pl.ds(0, NZ - 1)])
    wait(send_sem, 3, core_in)
    wait(send_sem, 4, stat_in.at[pl.ds(0, PLANE - 1)])
    for v in range(2):
        wait(send_sem, 5 + v, grad_out.at[pl.ds(0, NZ - 1), v])


def per_device(first_view, second_view):
    row_count, feature_width = first_view.shape
    half = feature_width // 2
    width = half // NZ
    rows = row_count * NZ
    total_rows = rows * PLANE
    bf16, f32 = jnp.bfloat16, jnp.float32
    out = jax.ShapeDtypeStruct((row_count, half), bf16)
    return pl.pallas_call(
        kernel,
        out_shape=(out, out),
        in_specs=[pl.BlockSpec(memory_space=pltpu.VMEM)] * 2,
        out_specs=(pl.BlockSpec(memory_space=pltpu.VMEM),) * 2,
        scratch_shapes=[
            pltpu.VMEM((NZ, 2, row_count, width), bf16),
            pltpu.VMEM((2, rows, width), bf16),
            pltpu.VMEM((PLANE, 2, rows, width), bf16),
            pltpu.VMEM((2, PLANE, rows, width), bf16),
            pltpu.VMEM((2, rows, total_rows), bf16),
            pltpu.VMEM((NZ, 2, rows, total_rows), bf16),
            pltpu.VMEM((2, rows, total_rows), f32),
            pltpu.VMEM((2, rows, total_rows), f32),
            pltpu.VMEM((2, width), f32),
            pltpu.VMEM((PLANE, 2, width), f32),
            pltpu.VMEM((NZ, 2, row_count, width), bf16),
            pltpu.SemaphoreType.DMA((7,)),
            pltpu.SemaphoreType.DMA((7,)),
        ],
        compiler_params=pltpu.CompilerParams(
            collective_id=0, has_side_effects=True, vmem_limit_bytes=32 << 20
        ),
        name="twins",
    )(first_view, second_view)


def solution(mesh):
    return jax.shard_map(
        per_device,
        mesh=mesh,
        in_specs=(P("batch", None), P("batch", None)),
        out_specs=(P("batch", "tile"), P("batch", "tile")),
        check_vma=False,
    )
```

time: 1040 us -> 40.3 us (0.04)
  the two profiles are of different devices: /device:TPU:0 before, /device:TPU:1 now
where the time goes in v1:
time: 40.3 us; the launch traced here: 40.1 us
  Pallas kernels  36.7 us (91%)
  local copies, waits for them, and re-layouts  2.72 us (7%)
  between operations  0.65 us (2%)
    pallas_call x1, Pallas kernels, per_device(): pl.pallas_call(kernel, out_shape=(out, out), in_specs=[pl.BlockSpec(memor...  36.7 us
    unnamed x6, local copies, waits for them, and re-layouts  2.72 us

profile of v1, /device:TPU:1, one launch (start us, length us, event | category | flops | bytes accessed | tf_op | source)
XLA Modules:
  0.0 40.1 jit_solution(16150914731768119118)
XLA Ops:
  0.6 0.0 copy-start
  0.6 0.7 %copy-done = bf16[2,8192]{1,0:T(2,128)(2,1)S(1)} copy-done((bf16[2,8192]{1,0:T(2,128)(2,1)S(1)}, bf16[2,8192]{1,0:T(2,128)(2,1)}, u32[]{:S(2)}) %copy-start) | copy-done | bytes 32792
  1.4 0.0 copy-start.1
  1.4 0.8 %copy-done.1 = bf16[2,8192]{1,0:T(2,128)(2,1)S(1)} copy-done((bf16[2,8192]{1,0:T(2,128)(2,1)S(1)}, bf16[2,8192]{1,0:T(2,128)(2,1)}, u32[]{:S(2)}) %copy-start.1) | copy-done | bytes 32792
  2.1 36.7 %twins.1 = (bf16[2,4096]{1,0:T(2,128)(2,1)S(1)}, bf16[2,4096]{1,0:T(2,128)(2,1)S(1)}) custom-call(bf16[2,8192]{1,0:T(2,128)(2,1)S(1)} %copy-done, bf16[2,8192]{1,0:T(2,128)(2,1)S(1)} %copy-done.1), custom_call_target="tpu_custom_call" | custom-call | tf_op jit(solution)/shard_map/twins/pallas_call | solution.py:186
  38.9 0.6 %copy.6 = bf16[2,4096]{1,0:T(2,128)(2,1)} copy(bf16[2,4096]{1,0:T(2,128)(2,1)S(1)} %get-tuple-element.4) | data formatting | bytes 32768
  39.5 0.6 %copy.7 = bf16[2,4096]{1,0:T(2,128)(2,1)} copy(bf16[2,4096]{1,0:T(2,128)(2,1)S(1)} %get-tuple-element.5) | data formatting | bytes 32768
Async XLA Ops:
  0.6 0.8 %copy-start = (bf16[2,8192]{1,0:T(2,128)(2,1)S(1)}, bf16[2,8192]{1,0:T(2,128)(2,1)}, u32[]{:S(2)}) copy-start(bf16[2,8192]{1,0:T(2,128)(2,1)} %first_ref.1) | copy-start | bytes 98308
  1.4 0.8 %copy-start.1 = (bf16[2,8192]{1,0:T(2,128)(2,1)S(1)}, bf16[2,8192]{1,0:T(2,128)(2,1)}, u32[]{:S(2)}) copy-start(bf16[2,8192]{1,0:T(2,128)(2,1)} %second_ref.1) | copy-start | bytes 98308

commit v2 on v1

v2 whole, which is shorter than its diff:
```python
import jax
import jax.numpy as jnp
from jax import lax
from jax.experimental import pallas as pl
from jax.experimental.pallas import tpu as pltpu
from jax.sharding import PartitionSpec as P

epsilon = 1e-05
decorrelation = 0.0051

NY, NZ, NX = 4, 8, 4
PLANE = NY * NX
CORES = 2
LANES = 128
MESH = pl.DeviceIdType.MESH


def kernel(
    first_ref,
    second_ref,
    grads_ref,
    stage,
    line,
    whole,
    norm,
    other,
    gram_out,
    gram_in,
    stat_out,
    stat_in,
    grad_out,
    load_sem,
    line_sem,
    send_sem,
    recv_sem,
):
    batch = lax.axis_index("batch")
    tile = lax.axis_index("tile")
    x = batch % NX
    z = (batch // NX) % NZ
    y = batch // (NX * NZ)
    slot = y * NX + x
    chunks, pair = line.shape[0], line.shape[2]
    rows = NZ * pair
    total_rows = rows * PLANE
    whole_rows = whole.reshape(PLANE, chunks, rows, LANES)
    grad_rows = grad_out.reshape(chunks, rows, LANES)

    def line_peer(k):
        return (y * NZ + (z + k) % NZ) * NX + x

    def plane_peer(j, i):
        return (((y + j) % NY) * NZ + z) * NX + (x + i) % NX

    line_steps = [4, 3, 5, 2, 6, 1, 7]
    plane_steps = [(j, i) for j in (2, 1, 3, 0) for i in (2, 1, 3, 0) if i or j]
    sibling = (batch, 1 - tile)

    @pl.when(tile == 0)
    def _():
        pltpu.make_async_copy(first_ref, stage, load_sem).start()

    @pl.when(tile == 1)
    def _():
        pltpu.make_async_copy(second_ref, stage, load_sem).start()

    barrier = pltpu.get_barrier_semaphore()
    greeted = [(line_peer(k), c) for k in line_steps for c in (tile, 1 - tile)]
    greeted += [(plane_peer(j, i), tile) for j, i in plane_steps] + [sibling]
    for device in greeted:
        pl.semaphore_signal(barrier, inc=1, device_id=device, device_id_type=MESH)
    pltpu.make_async_copy(stage, stage, load_sem).wait()
    line[:, z] = stage[pl.ds(z * chunks, chunks)]
    pl.semaphore_wait(barrier, len(greeted))

    def send(phase, source, target, device, arrived=None):
        pltpu.make_async_remote_copy(
            src_ref=source,
            dst_ref=target,
            send_sem=send_sem.at[phase],
            recv_sem=recv_sem.at[phase] if arrived is None else arrived,
            device_id=device,
            device_id_type=MESH,
        ).start()

    def wait(sem, like):
        pltpu.make_async_copy(like, like, sem).wait()

    for k in line_steps:
        source = stage.at[pl.ds((z + k) % NZ * chunks, chunks)]
        send(0, source, line.at[:, z], (line_peer(k), tile), line_sem.at[k])
    for k in [0, 1, 7, 2, 6, 3, 5, 4]:
        origin = (z + NZ - k) % NZ
        piece = line.at[:, origin]
        if k:
            wait(line_sem.at[k], piece)
        for j, i in plane_steps:
            send(1, piece, whole.at[slot, :, origin], (plane_peer(j, i), tile))
    whole[slot] = line[...]
    wait(recv_sem.at[1], whole.at[pl.ds(0, PLANE - 1)])

    inverse = []
    for c in range(chunks):
        values = whole_rows[:, c].reshape(total_rows, LANES).astype(jnp.float32)
        mean = jnp.sum(values, 0, keepdims=True) / total_rows
        centered = values - mean
        variance = jnp.sum(centered * centered, 0, keepdims=True) / total_rows
        inverse.append(lax.rsqrt(variance + epsilon))
        norm[:, :, c * LANES : (c + 1) * LANES] = (
            (centered * inverse[c]).astype(jnp.bfloat16).reshape(PLANE, rows, LANES)
        )
    inverse = jnp.concatenate(inverse, 1)
    width = chunks * LANES
    gram_out[...] = lax.dot_general(
        norm[slot],
        norm[...].reshape(total_rows, width),
        (((1,), (1,)), ((), ())),
        preferred_element_type=jnp.float32,
    ).astype(jnp.bfloat16)

    for k in line_steps:
        send(2, gram_out, gram_in.at[z], (line_peer(k), 1 - tile))
    send(2, gram_out, gram_in.at[z], sibling)
    send(3, norm, other, sibling)
    wait(recv_sem.at[3], other)
    paired = []
    for c in range(chunks):
        lanes = slice(c * LANES, (c + 1) * LANES)
        product = norm[:, :, lanes].astype(jnp.float32) * other[:, :, lanes].astype(jnp.float32)
        paired.append(jnp.sum(product.reshape(total_rows, LANES), 0, keepdims=True))
    paired = jnp.concatenate(paired, 1) / total_rows
    excess = (paired - 1.0) - decorrelation * paired
    mine = norm[slot].astype(jnp.float32)
    direct = excess * other[slot].astype(jnp.float32)
    wait(recv_sem.at[2], gram_in)
    gram = jnp.sum(gram_in[...].astype(jnp.float32), 0) * (decorrelation / total_rows)
    high = gram.astype(jnp.bfloat16)
    low = (gram - high.astype(jnp.float32)).astype(jnp.bfloat16)
    both = jnp.dot(
        jnp.concatenate([high, low], 0),
        norm[...].reshape(total_rows, width),
        preferred_element_type=jnp.float32,
    )
    pull = both[:rows] + both[rows:] + direct
    stat_out[...] = jnp.sum(pull * mine, 0, keepdims=True)

    for j, i in plane_steps:
        send(4, stat_out, stat_in.at[slot], (plane_peer(j, i), tile))
    stat_in[slot] = stat_out[...]
    wait(recv_sem.at[4], stat_in.at[pl.ds(0, PLANE - 1)])
    stat = jnp.sum(stat_in[...], 0) / total_rows
    grad = (inverse * (pull - mine * stat)).astype(jnp.bfloat16)
    for c in range(chunks):
        grad_rows[c] = grad[:, c * LANES : (c + 1) * LANES]

    owner = z // (NZ // CORES)
    target = grads_ref.at[tile, pl.ds(z % (NZ // CORES) * chunks, chunks)]
    for k in line_steps:
        send(5, grad_out.at[:, (z + k) % NZ], target, (line_peer(k), owner))

    @pl.when(owner == tile)
    def _():
        pltpu.make_async_copy(grad_out.at[:, z], target, recv_sem.at[5]).start()

    @pl.when(owner != tile)
    def _():
        send(6, grad_out.at[:, z], target, sibling, recv_sem.at[5])

    wait(recv_sem.at[5], grads_ref)

    wait(send_sem.at[0], line.at[:, pl.ds(0, NZ - 1)])
    wait(send_sem.at[1], whole.at[pl.ds(0, PLANE - 1)])
    wait(send_sem.at[2], gram_in)
    wait(send_sem.at[3], other)
    wait(send_sem.at[4], stat_in.at[pl.ds(0, PLANE - 1)])
    wait(send_sem.at[5], grad_out.at[:, pl.ds(0, NZ - 1)])

    @pl.when(owner != tile)
    def _():
        wait(send_sem.at[6], grad_out.at[:, 0])


def per_device(first_view, second_view):
    row_count, feature_width = first_view.shape
    chunks = feature_width // (NZ * LANES)
    width = chunks * LANES
    rows = row_count * NZ
    total_rows = rows * PLANE
    half = feature_width // CORES
    bf16, f32 = jnp.bfloat16, jnp.float32
    views = [
        view.reshape(row_count, feature_width // LANES, LANES).transpose(1, 0, 2)
        for view in (first_view, second_view)
    ]
    grads = pl.pallas_call(
        kernel,
        out_shape=jax.ShapeDtypeStruct((2, half // LANES, row_count, LANES), bf16),
        in_specs=[pl.BlockSpec(memory_space=pltpu.HBM)] * 2,
        out_specs=pl.BlockSpec(memory_space=pltpu.VMEM),
        scratch_shapes=[
            pltpu.VMEM((feature_width // LANES, row_count, LANES), bf16),
            pltpu.VMEM((chunks, NZ, row_count, LANES), bf16),
            pltpu.VMEM((PLANE, chunks, NZ, row_count, LANES), bf16),
            pltpu.VMEM((PLANE, rows, width), bf16),
            pltpu.VMEM((PLANE, rows, width), bf16),
            pltpu.VMEM((rows, total_rows), bf16),
            pltpu.VMEM((NZ, rows, total_rows), bf16),
            pltpu.VMEM((1, width), f32),
            pltpu.VMEM((PLANE, 1, width), f32),
            pltpu.VMEM((chunks, NZ, row_count, LANES), bf16),
            pltpu.SemaphoreType.DMA,
            pltpu.SemaphoreType.DMA((NZ,)),
            pltpu.SemaphoreType.DMA((7,)),
            pltpu.SemaphoreType.DMA((6,)),
        ],
        compiler_params=pltpu.CompilerParams(
            collective_id=0, has_side_effects=True, vmem_limit_bytes=32 << 20
        ),
        name="twins",
    )(*[pltpu.with_memory_space_constraint(view, pltpu.HBM) for view in views])
    return tuple(grads[v].transpose(1, 0, 2).reshape(row_count, half) for v in range(2))


def solution(mesh):
    return jax.shard_map(
        per_device,
        mesh=mesh,
        in_specs=(P("batch", None), P("batch", None)),
        out_specs=(P("batch", "tile"), P("batch", "tile")),
        check_vma=False,
    )
```

time: 40.3 us -> 37.6 us (0.933)
  local copies, waits for them, and re-layouts: 2.72 us -> 0.64 us
  Pallas kernels: 36.7 us -> 36.1 us
    unnamed x6 -> x0, local copies, waits for them, and re-layouts: 2.72 us -> none
    reshape x0 -> x1, local copies, waits for them, and re-layouts: none -> 0.64 us  [per_device(): grads[v].transpose(1, 0, 2).reshape(row_count, half)]
    pallas_call x1, Pallas kernels: 36.7 us -> 36.1 us  [per_device(): pl.pallas_call(kernel, out_shape=jax.ShapeDtypeStruct((2, half // LANES,...]
where the time goes in v2:
time: 37.6 us; the launch traced here: 37.4 us
  Pallas kernels  36.1 us (96%)
  local copies, waits for them, and re-layouts  0.64 us (2%)
  between operations  0.64 us (2%)
    pallas_call x1, Pallas kernels, per_device(): pl.pallas_call(kernel, out_shape=jax.ShapeDtypeStruct((2, half // LANES,...  36.1 us

profile of v2, /device:TPU:1, one launch (start us, length us, event | category | flops | bytes accessed | tf_op | source)
XLA Modules:
  0.0 37.4 jit_solution(3402446405269618043)
XLA Ops:
  0.6 36.1 %twins.1 = bf16[2,32,2,128]{3,2,1,0:T(2,128)(2,1)S(1)} custom-call(bf16[64,2,128]{2,1,0:T(2,128)(2,1)} %bitcast.18, bf16[64,2,128]{2,1,0:T(2,128)(2,1)} %bitcast.19), custom_call_target="tpu_custom_call" | custom-call | tf_op jit(solution)/shard_map/twins/pallas_call | solution.py:195
  36.8 0.6 %slice_bitcast_fusion = (bf16[2,4096]{1,0:T(2,128)(2,1)}, bf16[2,4096]{1,0:T(2,128)(2,1)}) fusion(bf16[2,32,2,128]{3,2,1,0:T(2,128)(2,1)S(1)} %twins.1), kind=kLoop, calls=%fused_computation | loop fusion | bytes 65536 | tf_op jit(solution)/shard_map/reshape | solution.py:221

commit v3 on v2

--- a/solution.py
+++ b/solution.py
@@ -52,6 +52,10 @@
     def plane_peer(j, i):
         return (((y + j) % NY) * NZ + z) * NX + (x + i) % NX
 
+    def block_of(k):
+        turned = (k + 1) % NZ
+        return (turned + NZ // 2) % NZ
+
     line_steps = [4, 3, 5, 2, 6, 1, 7]
     plane_steps = [(j, i) for j in (2, 1, 3, 0) for i in (2, 1, 3, 0) if i or j]
     sibling = (batch, 1 - tile)
@@ -70,7 +74,7 @@
     for device in greeted:
         pl.semaphore_signal(barrier, inc=1, device_id=device, device_id_type=MESH)
     pltpu.make_async_copy(stage, stage, load_sem).wait()
-    line[:, z] = stage[pl.ds(z * chunks, chunks)]
+    line[:, z] = stage[pl.ds(block_of(z) * chunks, chunks)]
     pl.semaphore_wait(barrier, len(greeted))
 
     def send(phase, source, target, device, arrived=None):
@@ -87,7 +91,7 @@
         pltpu.make_async_copy(like, like, sem).wait()
 
     for k in line_steps:
-        source = stage.at[pl.ds((z + k) % NZ * chunks, chunks)]
+        source = stage.at[pl.ds(block_of((z + k) % NZ) * chunks, chunks)]
         send(0, source, line.at[:, z], (line_peer(k), tile), line_sem.at[k])
     for k in [0, 1, 7, 2, 6, 3, 5, 4]:
         origin = (z + NZ - k) % NZ
@@ -153,8 +157,8 @@
     for c in range(chunks):
         grad_rows[c] = grad[:, c * LANES : (c + 1) * LANES]
 
-    owner = z // (NZ // CORES)
-    target = grads_ref.at[tile, pl.ds(z % (NZ // CORES) * chunks, chunks)]
+    owner = block_of(z) // (NZ // CORES)
+    target = grads_ref.at[tile, pl.ds(block_of(z) % (NZ // CORES) * chunks, chunks)]
     for k in line_steps:
         send(5, grad_out.at[:, (z + k) % NZ], target, (line_peer(k), owner))
 

time: 37.6 us -> 35.9 us (0.955)
  Pallas kernels: 36.1 us -> 34.4 us
    pallas_call x1, Pallas kernels: 36.1 us -> 34.4 us  [per_device(): pl.pallas_call(kernel, out_shape=jax.ShapeDtypeStruct((2, half // LANES,...]
where the time goes in v3:
time: 35.9 us; the launch traced here: 35.7 us
  Pallas kernels  34.4 us (96%)
  local copies, waits for them, and re-layouts  0.64 us (2%)
  between operations  0.64 us (2%)
    pallas_call x1, Pallas kernels, per_device(): pl.pallas_call(kernel, out_shape=jax.ShapeDtypeStruct((2, half // LANES,...  34.4 us

profile of v3, /device:TPU:1, one launch (start us, length us, event | category | flops | bytes accessed | tf_op | source)
XLA Modules:
  0.0 35.7 jit_solution(11012786685894158662)
XLA Ops:
  0.6 34.4 %twins.1 = bf16[2,32,2,128]{3,2,1,0:T(2,128)(2,1)S(1)} custom-call(bf16[64,2,128]{2,1,0:T(2,128)(2,1)} %bitcast.18, bf16[64,2,128]{2,1,0:T(2,128)(2,1)} %bitcast.19), custom_call_target="tpu_custom_call" | custom-call | tf_op jit(solution)/shard_map/twins/pallas_call | solution.py:199
  35.1 0.6 %slice_bitcast_fusion = (bf16[2,4096]{1,0:T(2,128)(2,1)}, bf16[2,4096]{1,0:T(2,128)(2,1)}) fusion(bf16[2,32,2,128]{3,2,1,0:T(2,128)(2,1)S(1)} %twins.1), kind=kLoop, calls=%fused_computation | loop fusion | bytes 65536 | tf_op jit(solution)/shard_map/reshape | solution.py:225

commit v4 on v3

--- a/solution.py
+++ b/solution.py
@@ -13,6 +13,13 @@
 CORES = 2
 LANES = 128
 MESH = pl.DeviceIdType.MESH
+
+
+def fold(values):
+    while values.shape[0] > 8:
+        half = values.shape[0] // 2
+        values = values[:half] + values[half:]
+    return jnp.sum(values, 0, keepdims=True)
 
 
 def kernel(
@@ -58,6 +65,8 @@
 
     line_steps = [4, 3, 5, 2, 6, 1, 7]
     plane_steps = [(j, i) for j in (2, 1, 3, 0) for i in (2, 1, 3, 0) if i or j]
+    far_steps = [(j, i) for j, i in plane_steps if min(j, NY - j) + min(i, NX - i) > 2]
+    near_steps = [step for step in plane_steps if step not in far_steps]
     sibling = (batch, 1 - tile)
 
     @pl.when(tile == 0)
@@ -74,7 +83,8 @@
     for device in greeted:
         pl.semaphore_signal(barrier, inc=1, device_id=device, device_id_type=MESH)
     pltpu.make_async_copy(stage, stage, load_sem).wait()
-    line[:, z] = stage[pl.ds(block_of(z) * chunks, chunks)]
+    own = stage.at[pl.ds(block_of(z) * chunks, chunks)]
+    pltpu.make_async_copy(own, line.at[:, z], line_sem.at[0]).start()
     pl.semaphore_wait(barrier, len(greeted))
 
     def send(phase, source, target, device, arrived=None):
@@ -93,25 +103,53 @@
     for k in line_steps:
         source = stage.at[pl.ds(block_of((z + k) % NZ) * chunks, chunks)]
         send(0, source, line.at[:, z], (line_peer(k), tile), line_sem.at[k])
-    for k in [0, 1, 7, 2, 6, 3, 5, 4]:
+    @pl.loop(0, NZ)
+    def _(n):
+        k = jnp.where(n % 2 == 1, (n + 1) // 2, (NZ - n // 2) % NZ)
         origin = (z + NZ - k) % NZ
         piece = line.at[:, origin]
-        if k:
-            wait(line_sem.at[k], piece)
+        wait(line_sem.at[k], piece)
         for j, i in plane_steps:
-            send(1, piece, whole.at[slot, :, origin], (plane_peer(j, i), tile))
-    whole[slot] = line[...]
-    wait(recv_sem.at[1], whole.at[pl.ds(0, PLANE - 1)])
-
-    inverse = []
+            send(
+                1,
+                piece,
+                whole.at[slot, :, origin],
+                (plane_peer(j, i), tile),
+                recv_sem.at[6 if (j, i) in far_steps else 1],
+            )
+
+    line_rows = line.reshape(chunks, rows, LANES)
+    shifts = [
+        jnp.sum(line_rows[c].astype(jnp.float32), 0, keepdims=True) / rows for c in range(chunks)
+    ]
+    sums = [jnp.zeros((8, LANES), jnp.float32)] * chunks
+    squares = [jnp.zeros((8, LANES), jnp.float32)] * chunks
+
+    def gather(source, block_rows):
+        for c in range(chunks):
+            block = block_rows[c]
+            norm[source, :, c * LANES : (c + 1) * LANES] = block
+            values = block.astype(jnp.float32) - shifts[c]
+            sums[c] += values[:8] + values[8:]
+            squares[c] += values[:8] * values[:8] + values[8:] * values[8:]
+
+    gather(slot, line_rows)
+    for sem, steps in ((1, near_steps), (6, far_steps)):
+        wait(recv_sem.at[sem], whole.at[pl.ds(0, len(steps))])
+        for j, i in steps:
+            source = (y + NY - j) % NY * NX + (x + NX - i) % NX
+            gather(source, whole_rows.at[source])
+    moves = [jnp.sum(v, 0, keepdims=True) / total_rows for v in sums]
+    means = [s + m for s, m in zip(shifts, moves)]
+    inverse = [
+        lax.rsqrt(jnp.sum(v, 0, keepdims=True) / total_rows - m * m + epsilon)
+        for v, m in zip(squares, moves)
+    ]
     for c in range(chunks):
-        values = whole_rows[:, c].reshape(total_rows, LANES).astype(jnp.float32)
-        mean = jnp.sum(values, 0, keepdims=True) / total_rows
-        centered = values - mean
-        variance = jnp.sum(centered * centered, 0, keepdims=True) / total_rows
-        inverse.append(lax.rsqrt(variance + epsilon))
-        norm[:, :, c * LANES : (c + 1) * LANES] = (
-            (centered * inverse[c]).astype(jnp.bfloat16).reshape(PLANE, rows, LANES)
+        lanes = slice(c * LANES, (c + 1) * LANES)
+        values = norm[:, :, lanes].reshape(total_rows, LANES).astype(jnp.float32)
+        norm[:, :, lanes] = (
+            ((values - means[c]) * inverse[c]).astype(jnp.bfloat16).reshape(PLANE, rows, LANES)
         )
     inverse = jnp.concatenate(inverse, 1)
     width = chunks * LANES
@@ -131,7 +169,7 @@
     for c in range(chunks):
         lanes = slice(c * LANES, (c + 1) * LANES)
         product = norm[:, :, lanes].astype(jnp.float32) * other[:, :, lanes].astype(jnp.float32)
-        paired.append(jnp.sum(product.reshape(total_rows, LANES), 0, keepdims=True))
+        paired.append(fold(product.reshape(total_rows, LANES)))
     paired = jnp.concatenate(paired, 1) / total_rows
     excess = (paired - 1.0) - decorrelation * paired
     mine = norm[slot].astype(jnp.float32)
@@ -146,7 +184,7 @@
         preferred_element_type=jnp.float32,
     )
     pull = both[:rows] + both[rows:] + direct
-    stat_out[...] = jnp.sum(pull * mine, 0, keepdims=True)
+    stat_out[...] = fold(pull * mine)
 
     for j, i in plane_steps:
         send(4, stat_out, stat_in.at[slot], (plane_peer(j, i), tile))
@@ -215,7 +253,7 @@
             pltpu.SemaphoreType.DMA,
             pltpu.SemaphoreType.DMA((NZ,)),
             pltpu.SemaphoreType.DMA((7,)),
-            pltpu.SemaphoreType.DMA((6,)),
+            pltpu.SemaphoreType.DMA((7,)),
         ],
         compiler_params=pltpu.CompilerParams(
             collective_id=0, has_side_effects=True, vmem_limit_bytes=32 << 20

time: 35.9 us -> 35.3 us (0.983)
  Pallas kernels: 34.4 us -> 33.8 us
    pallas_call x1, Pallas kernels: 34.4 us -> 33.8 us  [per_device(): pl.pallas_call(kernel, out_shape=jax.ShapeDtypeStruct((2, half // LANES,...]
where the time goes in v4:
time: 35.3 us; the launch traced here: 35 us
  Pallas kernels  33.8 us (96%)
  local copies, waits for them, and re-layouts  0.64 us (2%)
  between operations  0.64 us (2%)
    pallas_call x1, Pallas kernels, per_device(): pl.pallas_call(kernel, out_shape=jax.ShapeDtypeStruct((2, half // LANES,...  33.8 us

profile of v4, /device:TPU:1, one launch (start us, length us, event | category | flops | bytes accessed | tf_op | source)
XLA Modules:
  0.0 35.0 jit_solution(17513941340271882713)
XLA Ops:
  0.6 33.8 %twins.1 = bf16[2,32,2,128]{3,2,1,0:T(2,128)(2,1)S(1)} custom-call(bf16[64,2,128]{2,1,0:T(2,128)(2,1)} %bitcast.18, bf16[64,2,128]{2,1,0:T(2,128)(2,1)} %bitcast.19), custom_call_target="tpu_custom_call" | custom-call | tf_op jit(solution)/shard_map/twins/pallas_call | solution.py:237
  34.4 0.6 %slice_bitcast_fusion = (bf16[2,4096]{1,0:T(2,128)(2,1)}, bf16[2,4096]{1,0:T(2,128)(2,1)}) fusion(bf16[2,32,2,128]{3,2,1,0:T(2,128)(2,1)S(1)} %twins.1), kind=kLoop, calls=%fused_computation | loop fusion | bytes 65536 | tf_op jit(solution)/shard_map/reshape | solution.py:263

commit v5 on v4

--- a/solution.py
+++ b/solution.py
@@ -145,20 +145,28 @@
         lax.rsqrt(jnp.sum(v, 0, keepdims=True) / total_rows - m * m + epsilon)
         for v, m in zip(squares, moves)
     ]
-    for c in range(chunks):
-        lanes = slice(c * LANES, (c + 1) * LANES)
-        values = norm[:, :, lanes].reshape(total_rows, LANES).astype(jnp.float32)
-        norm[:, :, lanes] = (
-            ((values - means[c]) * inverse[c]).astype(jnp.bfloat16).reshape(PLANE, rows, LANES)
+    def normalized(values, c):
+        return ((values.astype(jnp.float32) - means[c]) * inverse[c]).astype(jnp.bfloat16)
+
+    width = chunks * LANES
+    gram, mine = jnp.zeros((rows, total_rows), jnp.float32), []
+    for c in range(0, chunks, 2):
+        pair_rows = []
+        for d in (c, c + 1):
+            lanes = slice(d * LANES, (d + 1) * LANES)
+            values = normalized(norm[:, :, lanes].reshape(total_rows, LANES), d)
+            norm[:, :, lanes] = values.reshape(PLANE, rows, LANES)
+            pair_rows.append(values)
+            mine.append(normalized(line_rows[d], d))
+        gram += lax.dot_general(
+            jnp.concatenate(mine[-2:], 1),
+            jnp.concatenate(pair_rows, 1),
+            (((1,), (1,)), ((), ())),
+            preferred_element_type=jnp.float32,
         )
     inverse = jnp.concatenate(inverse, 1)
-    width = chunks * LANES
-    gram_out[...] = lax.dot_general(
-        norm[slot],
-        norm[...].reshape(total_rows, width),
-        (((1,), (1,)), ((), ())),
-        preferred_element_type=jnp.float32,
-    ).astype(jnp.bfloat16)
+    mine = jnp.concatenate(mine, 1).astype(jnp.float32)
+    gram_out[...] = gram.astype(jnp.bfloat16)
 
     for k in line_steps:
         send(2, gram_out, gram_in.at[z], (line_peer(k), 1 - tile))
@@ -172,7 +180,6 @@
         paired.append(fold(product.reshape(total_rows, LANES)))
     paired = jnp.concatenate(paired, 1) / total_rows
     excess = (paired - 1.0) - decorrelation * paired
-    mine = norm[slot].astype(jnp.float32)
     direct = excess * other[slot].astype(jnp.float32)
     wait(recv_sem.at[2], gram_in)
     gram = jnp.sum(gram_in[...].astype(jnp.float32), 0) * (decorrelation / total_rows)
@@ -184,16 +191,19 @@
         preferred_element_type=jnp.float32,
     )
     pull = both[:rows] + both[rows:] + direct
-    stat_out[...] = fold(pull * mine)
+    stat = fold(pull * mine)
+    for c in range(chunks):
+        stat_out[c : c + 1] = stat[:, c * LANES : (c + 1) * LANES]
 
     for j, i in plane_steps:
         send(4, stat_out, stat_in.at[slot], (plane_peer(j, i), tile))
     stat_in[slot] = stat_out[...]
     wait(recv_sem.at[4], stat_in.at[pl.ds(0, PLANE - 1)])
     stat = jnp.sum(stat_in[...], 0) / total_rows
-    grad = (inverse * (pull - mine * stat)).astype(jnp.bfloat16)
     for c in range(chunks):
-        grad_rows[c] = grad[:, c * LANES : (c + 1) * LANES]
+        lanes = slice(c * LANES, (c + 1) * LANES)
+        grad = inverse[:, lanes] * (pull[:, lanes] - mine[:, lanes] * stat[c : c + 1])
+        grad_rows[c] = grad.astype(jnp.bfloat16)
 
     owner = block_of(z) // (NZ // CORES)
     target = grads_ref.at[tile, pl.ds(block_of(z) % (NZ // CORES) * chunks, chunks)]
@@ -247,8 +257,8 @@
             pltpu.VMEM((PLANE, rows, width), bf16),
             pltpu.VMEM((rows, total_rows), bf16),
             pltpu.VMEM((NZ, rows, total_rows), bf16),
-            pltpu.VMEM((1, width), f32),
-            pltpu.VMEM((PLANE, 1, width), f32),
+            pltpu.VMEM((chunks, LANES), f32),
+            pltpu.VMEM((PLANE, chunks, LANES), f32),
             pltpu.VMEM((chunks, NZ, row_count, LANES), bf16),
             pltpu.SemaphoreType.DMA,
             pltpu.SemaphoreType.DMA((NZ,)),

time: 35.3 us -> 35.1 us (level)
  no operation moved by 1% of the time
where the time goes in v5:
time: 35.1 us; the launch traced here: 34.8 us
  Pallas kernels  33.6 us (96%)
  local copies, waits for them, and re-layouts  0.64 us (2%)
  between operations  0.64 us (2%)
    pallas_call x1, Pallas kernels, per_device(): pl.pallas_call(kernel, out_shape=jax.ShapeDtypeStruct((2, half // LANES,...  33.6 us

profile of v5, /device:TPU:1, one launch (start us, length us, event | category | flops | bytes accessed | tf_op | source)
XLA Modules:
  0.0 34.8 jit_solution(9626662789966661735)
XLA Ops:
  0.6 33.6 %twins.1 = bf16[2,32,2,128]{3,2,1,0:T(2,128)(2,1)S(1)} custom-call(bf16[64,2,128]{2,1,0:T(2,128)(2,1)} %bitcast.18, bf16[64,2,128]{2,1,0:T(2,128)(2,1)} %bitcast.19), custom_call_target="tpu_custom_call" | custom-call | tf_op jit(solution)/shard_map/twins/pallas_call | solution.py:247
  34.2 0.6 %slice_bitcast_fusion = (bf16[2,4096]{1,0:T(2,128)(2,1)}, bf16[2,4096]{1,0:T(2,128)(2,1)}) fusion(bf16[2,32,2,128]{3,2,1,0:T(2,128)(2,1)S(1)} %twins.1), kind=kLoop, calls=%fused_computation | loop fusion | bytes 65536 | tf_op jit(solution)/shard_map/reshape | solution.py:273

commit v6 on v5

--- a/solution.py
+++ b/solution.py
@@ -69,19 +69,19 @@
     near_steps = [step for step in plane_steps if step not in far_steps]
     sibling = (batch, 1 - tile)
 
-    @pl.when(tile == 0)
-    def _():
-        pltpu.make_async_copy(first_ref, stage, load_sem).start()
-
-    @pl.when(tile == 1)
-    def _():
-        pltpu.make_async_copy(second_ref, stage, load_sem).start()
-
     barrier = pltpu.get_barrier_semaphore()
-    greeted = [(line_peer(k), c) for k in line_steps for c in (tile, 1 - tile)]
+    greeted = [(line_peer(k), tile) for k in line_steps]
     greeted += [(plane_peer(j, i), tile) for j, i in plane_steps] + [sibling]
     for device in greeted:
         pl.semaphore_signal(barrier, inc=1, device_id=device, device_id_type=MESH)
+    @pl.when(tile == 0)
+    def _():
+        pltpu.make_async_copy(first_ref, stage, load_sem).start()
+
+    @pl.when(tile == 1)
+    def _():
+        pltpu.make_async_copy(second_ref, stage, load_sem).start()
+
     pltpu.make_async_copy(stage, stage, load_sem).wait()
     own = stage.at[pl.ds(block_of(z) * chunks, chunks)]
     pltpu.make_async_copy(own, line.at[:, z], line_sem.at[0]).start()

time: 35.1 us -> 35 us (level)
  no operation moved by 1% of the time
where the time goes in v6:
time: 35 us; the launch traced here: 34.7 us
  Pallas kernels  33.4 us (95%)
  local copies, waits for them, and re-layouts  0.64 us (2%)
  between operations  0.64 us (2%)
    pallas_call x1, Pallas kernels, per_device(): pl.pallas_call(kernel, out_shape=jax.ShapeDtypeStruct((2, half // LANES,...  33.4 us

profile of v6, /device:TPU:1, one launch (start us, length us, event | category | flops | bytes accessed | tf_op | source)
XLA Modules:
  0.0 34.7 jit_solution(16998676561705624188)
XLA Ops:
  0.6 33.4 %twins.1 = bf16[2,32,2,128]{3,2,1,0:T(2,128)(2,1)S(1)} custom-call(bf16[64,2,128]{2,1,0:T(2,128)(2,1)} %bitcast.18, bf16[64,2,128]{2,1,0:T(2,128)(2,1)} %bitcast.19), custom_call_target="tpu_custom_call" | custom-call | tf_op jit(solution)/shard_map/twins/pallas_call | solution.py:247
  34.0 0.6 %slice_bitcast_fusion = (bf16[2,4096]{1,0:T(2,128)(2,1)}, bf16[2,4096]{1,0:T(2,128)(2,1)}) fusion(bf16[2,32,2,128]{3,2,1,0:T(2,128)(2,1)S(1)} %twins.1), kind=kLoop, calls=%fused_computation | loop fusion | bytes 65536 | tf_op jit(solution)/shard_map/reshape | solution.py:273

commit v7 on v5

--- a/solution.py
+++ b/solution.py
@@ -196,29 +196,34 @@
         stat_out[c : c + 1] = stat[:, c * LANES : (c + 1) * LANES]
 
     for j, i in plane_steps:
-        send(4, stat_out, stat_in.at[slot], (plane_peer(j, i), tile))
-    stat_in[slot] = stat_out[...]
-    wait(recv_sem.at[4], stat_in.at[pl.ds(0, PLANE - 1)])
-    stat = jnp.sum(stat_in[...], 0) / total_rows
+        arrived = recv_sem.at[5 if (j, i) in far_steps else 4]
+        send(4, stat_out, stat_in.at[slot], (plane_peer(j, i), tile), arrived)
+    scaled_pull, scaled_mine = inverse * pull, inverse * mine
+    stat = stat_out[...]
+    for sem, steps in ((4, near_steps), (5, far_steps)):
+        wait(recv_sem.at[sem], stat_in.at[pl.ds(0, len(steps))])
+        for j, i in steps:
+            stat += stat_in[(y + NY - j) % NY * NX + (x + NX - i) % NX]
+    stat = stat / total_rows
     for c in range(chunks):
         lanes = slice(c * LANES, (c + 1) * LANES)
-        grad = inverse[:, lanes] * (pull[:, lanes] - mine[:, lanes] * stat[c : c + 1])
+        grad = scaled_pull[:, lanes] - scaled_mine[:, lanes] * stat[c : c + 1]
         grad_rows[c] = grad.astype(jnp.bfloat16)
 
     owner = block_of(z) // (NZ // CORES)
     target = grads_ref.at[tile, pl.ds(block_of(z) % (NZ // CORES) * chunks, chunks)]
     for k in line_steps:
-        send(5, grad_out.at[:, (z + k) % NZ], target, (line_peer(k), owner))
+        send(5, grad_out.at[:, (z + k) % NZ], target, (line_peer(k), owner), recv_sem.at[7])
 
     @pl.when(owner == tile)
     def _():
-        pltpu.make_async_copy(grad_out.at[:, z], target, recv_sem.at[5]).start()
+        pltpu.make_async_copy(grad_out.at[:, z], target, recv_sem.at[7]).start()
 
     @pl.when(owner != tile)
     def _():
-        send(6, grad_out.at[:, z], target, sibling, recv_sem.at[5])
-
-    wait(recv_sem.at[5], grads_ref)
+        send(6, grad_out.at[:, z], target, sibling, recv_sem.at[7])
+
+    wait(recv_sem.at[7], grads_ref)
 
     wait(send_sem.at[0], line.at[:, pl.ds(0, NZ - 1)])
     wait(send_sem.at[1], whole.at[pl.ds(0, PLANE - 1)])
@@ -263,7 +268,7 @@
             pltpu.SemaphoreType.DMA,
             pltpu.SemaphoreType.DMA((NZ,)),
             pltpu.SemaphoreType.DMA((7,)),
-            pltpu.SemaphoreType.DMA((7,)),
+            pltpu.SemaphoreType.DMA((8,)),
         ],
         compiler_params=pltpu.CompilerParams(
             collective_id=0, has_side_effects=True, vmem_limit_bytes=32 << 20

time: 35.1 us -> 35.1 us (level)
  no operation moved by 1% of the time
where the time goes in v7:
time: 35.1 us; the launch traced here: 34.8 us
  Pallas kernels  33.6 us (96%)
  local copies, waits for them, and re-layouts  0.64 us (2%)
  between operations  0.64 us (2%)
    pallas_call x1, Pallas kernels, per_device(): pl.pallas_call(kernel, out_shape=jax.ShapeDtypeStruct((2, half // LANES,...  33.6 us

profile of v7, /device:TPU:1, one launch (start us, length us, event | category | flops | bytes accessed | tf_op | source)
XLA Modules:
  0.0 34.8 jit_solution(2251801514923235629)
XLA Ops:
  0.6 33.6 %twins.1 = bf16[2,32,2,128]{3,2,1,0:T(2,128)(2,1)S(1)} custom-call(bf16[64,2,128]{2,1,0:T(2,128)(2,1)} %bitcast.18, bf16[64,2,128]{2,1,0:T(2,128)(2,1)} %bitcast.19), custom_call_target="tpu_custom_call" | custom-call | tf_op jit(solution)/shard_map/twins/pallas_call | solution.py:252
  34.2 0.6 %slice_bitcast_fusion = (bf16[2,4096]{1,0:T(2,128)(2,1)}, bf16[2,4096]{1,0:T(2,128)(2,1)}) fusion(bf16[2,32,2,128]{3,2,1,0:T(2,128)(2,1)S(1)} %twins.1), kind=kLoop, calls=%fused_computation | loop fusion | bytes 65536 | tf_op jit(solution)/shard_map/reshape | solution.py:278

commit v8 on v7

--- a/solution.py
+++ b/solution.py
@@ -69,19 +69,19 @@
     near_steps = [step for step in plane_steps if step not in far_steps]
     sibling = (batch, 1 - tile)
 
-    @pl.when(tile == 0)
-    def _():
-        pltpu.make_async_copy(first_ref, stage, load_sem).start()
-
-    @pl.when(tile == 1)
-    def _():
-        pltpu.make_async_copy(second_ref, stage, load_sem).start()
-
     barrier = pltpu.get_barrier_semaphore()
-    greeted = [(line_peer(k), c) for k in line_steps for c in (tile, 1 - tile)]
+    greeted = [(line_peer(k), tile) for k in line_steps]
     greeted += [(plane_peer(j, i), tile) for j, i in plane_steps] + [sibling]
     for device in greeted:
         pl.semaphore_signal(barrier, inc=1, device_id=device, device_id_type=MESH)
+    @pl.when(tile == 0)
+    def _():
+        pltpu.make_async_copy(first_ref, stage, load_sem).start()
+
+    @pl.when(tile == 1)
+    def _():
+        pltpu.make_async_copy(second_ref, stage, load_sem).start()
+
     pltpu.make_async_copy(stage, stage, load_sem).wait()
     own = stage.at[pl.ds(block_of(z) * chunks, chunks)]
     pltpu.make_async_copy(own, line.at[:, z], line_sem.at[0]).start()

time: 35.1 us -> 35 us (level)
  no operation moved by 1% of the time
where the time goes in v8:
time: 35 us; the launch traced here: 34.7 us
  Pallas kernels  33.4 us (95%)
  local copies, waits for them, and re-layouts  0.64 us (2%)
  between operations  0.64 us (2%)
    pallas_call x1, Pallas kernels, per_device(): pl.pallas_call(kernel, out_shape=jax.ShapeDtypeStruct((2, half // LANES,...  33.4 us

profile of v8, /device:TPU:1, one launch (start us, length us, event | category | flops | bytes accessed | tf_op | source)
XLA Modules:
  0.0 34.7 jit_solution(17406507856358480828)
XLA Ops:
  0.6 33.4 %twins.1 = bf16[2,32,2,128]{3,2,1,0:T(2,128)(2,1)S(1)} custom-call(bf16[64,2,128]{2,1,0:T(2,128)(2,1)} %bitcast.18, bf16[64,2,128]{2,1,0:T(2,128)(2,1)} %bitcast.19), custom_call_target="tpu_custom_call" | custom-call | tf_op jit(solution)/shard_map/twins/pallas_call | solution.py:252
  34.0 0.6 %slice_bitcast_fusion = (bf16[2,4096]{1,0:T(2,128)(2,1)}, bf16[2,4096]{1,0:T(2,128)(2,1)}) fusion(bf16[2,32,2,128]{3,2,1,0:T(2,128)(2,1)S(1)} %twins.1), kind=kLoop, calls=%fused_computation | loop fusion | bytes 65536 | tf_op jit(solution)/shard_map/reshape | solution.py:278

commit v9 on v8

--- a/solution.py
+++ b/solution.py
@@ -65,6 +65,7 @@
 
     line_steps = [4, 3, 5, 2, 6, 1, 7]
     plane_steps = [(j, i) for j in (2, 1, 3, 0) for i in (2, 1, 3, 0) if i or j]
+    plane_steps.sort(key=lambda s: -min(s[0], NY - s[0]) - min(s[1], NX - s[1]))
     far_steps = [(j, i) for j, i in plane_steps if min(j, NY - j) + min(i, NX - i) > 2]
     near_steps = [step for step in plane_steps if step not in far_steps]
     sibling = (batch, 1 - tile)

time: 35 us -> 35 us (level)
  no operation moved by 1% of the time
where the time goes in v9:
time: 35 us; the launch traced here: 34.7 us
  Pallas kernels  33.4 us (95%)
  local copies, waits for them, and re-layouts  0.64 us (2%)
  between operations  0.64 us (2%)
    pallas_call x1, Pallas kernels, per_device(): pl.pallas_call(kernel, out_shape=jax.ShapeDtypeStruct((2, half // LANES,...  33.4 us

profile of v9, /device:TPU:1, one launch (start us, length us, event | category | flops | bytes accessed | tf_op | source)
XLA Modules:
  0.0 34.7 jit_solution(481645983952005704)
XLA Ops:
  0.6 33.4 %twins.1 = bf16[2,32,2,128]{3,2,1,0:T(2,128)(2,1)S(1)} custom-call(bf16[64,2,128]{2,1,0:T(2,128)(2,1)} %bitcast.18, bf16[64,2,128]{2,1,0:T(2,128)(2,1)} %bitcast.19), custom_call_target="tpu_custom_call" | custom-call | tf_op jit(solution)/shard_map/twins/pallas_call | solution.py:253
  34.0 0.6 %slice_bitcast_fusion = (bf16[2,4096]{1,0:T(2,128)(2,1)}, bf16[2,4096]{1,0:T(2,128)(2,1)}) fusion(bf16[2,32,2,128]{3,2,1,0:T(2,128)(2,1)S(1)} %twins.1), kind=kLoop, calls=%fused_computation | loop fusion | bytes 65536 | tf_op jit(solution)/shard_map/reshape | solution.py:279
